TPU v7x, 512 devices: a whole 4x4x16 slice. The times are simulated.
512 devices in a mesh: dp: 8 (over y, core), expert: 64 (over x, z).
Axes of the slice: x: 4, y: 4, z: 16, core: 2. Of those that a mesh axis runs over, the one named last changes fastest.
Arguments:
- tokens: bfloat16 [32768, 1024], P(('dp', 'expert')), may hold values from -6 to 6
- expert_ids: int32 [32768, 8], P(('dp', 'expert')), may hold values from 0 to 63, all different within a row; in each aligned block of 64 rows (0 to 63, 64 to 127, ...) at most 10 rows name the same one
- route_weight: float32 [32768, 8], P(('dp', 'expert')), may hold values from 0.05 to 0.5
- out_grad: bfloat16 [32768, 1024], P(('dp', 'expert')), may hold values from -6 to 6
- gate_weight: bfloat16 [64, 1024, 384], P('expert', 'dp'), may hold values from -0.1875 to 0.1875
- up_weight: bfloat16 [64, 1024, 384], P('expert', 'dp'), may hold values from -0.1875 to 0.1875
- down_weight: bfloat16 [64, 384, 1024], P('expert', None, 'dp'), may hold values from -0.3125 to 0.3125
Outputs:
- layer_out: bfloat16 [32768, 1024], P(('dp', 'expert'))
- token_grad: bfloat16 [32768, 1024], P(('dp', 'expert'))
- route_grad: float32 [32768, 8], P(('dp', 'expert'))
- gate_grad: float32 [64, 1024, 384], P('expert', 'dp')
- up_grad: float32 [64, 1024, 384], P('expert', 'dp')
- down_grad: float32 [64, 384, 1024], P('expert', None, 'dp')
Inputs may be any that keep to these rules, and one draw needn't show every extreme that they name: `expert_ids`: each token names 8 different experts. Among the 64 tokens of one device no expert is named by more than 10 tokens, and in every draw some expert is named by exactly 10 tokens of some device.
All inputs are finite; a program needn't handle non-finite values.
Results may differ from a plain program's by a relative error of at most 0.012.
Values may be sent and summed in bfloat16 or wider, within the bound.
No kernel may reach another device: no remote copies, remote signals or barrier semaphores. Data moves between devices by JAX's collectives and lax.ppermute only.
A program may use at most 64 MiB of HBM per device.

v0:
```python
import jax
import jax.numpy as jnp
from jax import lax
from jax.sharding import PartitionSpec as P


def layout(live_counts, slot_cap, padded_rows):
    owners = live_counts.shape[0]
    ends = jnp.cumsum(live_counts).astype(jnp.int32)
    starts = ends - live_counts
    total = ends[owners - 1]
    positions = jnp.arange(padded_rows, dtype=jnp.int32)
    source = jnp.minimum(
        jnp.sum((positions[:, None] >= ends[None, :]).astype(jnp.int32), 1), owners - 1
    )
    matches = source[:, None] == jnp.arange(owners, dtype=jnp.int32)[None, :]
    offset = positions - jnp.sum(jnp.where(matches, starts[None, :], 0), 1)
    valid = positions < total
    pick_rows = jnp.where(valid, source * slot_cap + offset, 0)
    slot_pos = jnp.arange(owners * slot_cap, dtype=jnp.int32) % slot_cap
    live_back = slot_pos < jnp.repeat(live_counts, slot_cap)
    back_rows = jnp.where(live_back, jnp.repeat(starts, slot_cap) + slot_pos, 0)
    return (pick_rows, valid, back_rows, live_back, total)


def compact(received, pick_rows, valid):
    feat_width = received.shape[2]
    rows = received.reshape(-1, feat_width)[pick_rows]
    return jnp.where(valid[:, None], rows, jnp.zeros_like(rows))


def spread(rows, back_rows, live_back, owners, slot_cap):
    picked = rows[back_rows]
    picked = jnp.where(live_back[:, None], picked, jnp.zeros_like(picked))
    return picked.reshape(owners, slot_cap, rows.shape[1])


def shards(tokens, expert_ids, route_weight, out_grad, gate_weight, up_weight, down_weight):
    block_rows = 128
    tok_rows, feat_width = tokens.shape
    top_picks = expert_ids.shape[1]
    hidden_units = gate_weight.shape[2]
    owners = lax.axis_size("expert")
    slot_cap = max(2, 5 * tok_rows * top_picks // (4 * owners))
    slot_total = owners * slot_cap
    padded_rows = -(-slot_total // block_rows) * block_rows
    flat_ids = expert_ids.reshape(-1)
    one_hot = (flat_ids[:, None] == jnp.arange(owners, dtype=jnp.int32)[None, :]).astype(jnp.int32)
    slot_rank = jnp.sum((jnp.cumsum(one_hot, 0) - one_hot) * one_hot, 1)
    pair_slots = flat_ids * slot_cap + slot_rank
    send_counts = jnp.sum(one_hot, 0).reshape(owners, 1)
    x_send = (
        jnp.zeros((slot_total, feat_width), jnp.bfloat16)
        .at[pair_slots]
        .set(jnp.repeat(tokens, top_picks, 0))
        .reshape(owners, slot_cap, feat_width)
    )
    pair_grad = (
        route_weight.reshape(-1, 1) * jnp.repeat(out_grad, top_picks, 0).astype(jnp.float32)
    ).astype(jnp.bfloat16)
    dy_send = (
        jnp.zeros((slot_total, feat_width), jnp.bfloat16)
        .at[pair_slots]
        .set(pair_grad)
        .reshape(owners, slot_cap, feat_width)
    )
    gate_full, up_full, down_full = (
        lax.all_gather(gate_weight, "dp", axis=1, tiled=True),
        lax.all_gather(up_weight, "dp", axis=1, tiled=True),
        lax.all_gather(down_weight, "dp", axis=2, tiled=True),
    )
    gate_full = gate_full[0]
    up_full = up_full[0]
    down_full = down_full[0]
    x_recv, recv_counts = (
        lax.all_to_all(x_send, "expert", split_axis=0, concat_axis=0, tiled=True),
        lax.all_to_all(send_counts, "expert", split_axis=0, concat_axis=0, tiled=True),
    )
    pick_rows, valid, back_rows, live_back, total = layout(recv_counts[:, 0], slot_cap, padded_rows)
    live_blocks = (total + block_rows - 1) // block_rows
    x_rows = compact(x_recv, pick_rows, valid)

    def forward_block(block_id, carry):
        y_buf, h_buf, g_buf, u_buf = carry
        row_start = block_id * block_rows
        x_blk = lax.dynamic_slice_in_dim(x_rows, row_start, block_rows, 0)
        gate_act = jnp.dot(x_blk, gate_full, preferred_element_type=jnp.float32)
        up_act = jnp.dot(x_blk, up_full, preferred_element_type=jnp.float32)
        hidden = (gate_act * jax.nn.sigmoid(gate_act) * up_act).astype(jnp.bfloat16)
        y_blk = jnp.dot(hidden, down_full, preferred_element_type=jnp.float32).astype(jnp.bfloat16)
        return (
            lax.dynamic_update_slice_in_dim(y_buf, y_blk, row_start, 0),
            lax.dynamic_update_slice_in_dim(h_buf, hidden, row_start, 0),
            lax.dynamic_update_slice_in_dim(g_buf, gate_act, row_start, 0),
            lax.dynamic_update_slice_in_dim(u_buf, up_act, row_start, 0),
        )

    forward_init = (
        jnp.zeros((padded_rows, feat_width), jnp.bfloat16),
        jnp.zeros((padded_rows, hidden_units), jnp.bfloat16),
        jnp.zeros((padded_rows, hidden_units), jnp.float32),
        jnp.zeros((padded_rows, hidden_units), jnp.float32),
    )
    y_rows, h_rows, g_rows, u_rows = lax.fori_loop(0, live_blocks, forward_block, forward_init)
    y_back = lax.all_to_all(
        spread(y_rows, back_rows, live_back, owners, slot_cap),
        "expert",
        split_axis=0,
        concat_axis=0,
        tiled=True,
    )
    dy_recv = lax.all_to_all(dy_send, "expert", split_axis=0, concat_axis=0, tiled=True)
    dy_rows = compact(dy_recv, pick_rows, valid)
    contract_last = (((1,), (1,)), ((), ()))
    contract_rows = (((0,), (0,)), ((), ()))

    def backward_block(block_id, carry):
        dx_buf, act_buf = carry
        row_start = block_id * block_rows
        dy_blk = lax.dynamic_slice_in_dim(dy_rows, row_start, block_rows, 0)
        gate_act = lax.dynamic_slice_in_dim(g_rows, row_start, block_rows, 0)
        up_act = lax.dynamic_slice_in_dim(u_rows, row_start, block_rows, 0)
        sigmoid_g = jax.nn.sigmoid(gate_act)
        hidden_grad = lax.dot_general(
            dy_blk, down_full, contract_last, preferred_element_type=jnp.float32
        )
        gate_back = (
            hidden_grad * up_act * sigmoid_g * (1.0 + gate_act * (1.0 - sigmoid_g))
        ).astype(jnp.bfloat16)
        up_back = (hidden_grad * gate_act * sigmoid_g).astype(jnp.bfloat16)
        dx_blk = (
            lax.dot_general(gate_back, gate_full, contract_last, preferred_element_type=jnp.float32)
            + lax.dot_general(up_back, up_full, contract_last, preferred_element_type=jnp.float32)
        ).astype(jnp.bfloat16)
        act_back = jnp.concatenate([gate_back, up_back], 1)
        return (
            lax.dynamic_update_slice_in_dim(dx_buf, dx_blk, row_start, 0),
            lax.dynamic_update_slice_in_dim(act_buf, act_back, row_start, 0),
        )

    backward_init = (
        jnp.zeros((padded_rows, feat_width), jnp.bfloat16),
        jnp.zeros((padded_rows, 2 * hidden_units), jnp.bfloat16),
    )
    dx_rows, act_rows = lax.fori_loop(0, live_blocks, backward_block, backward_init)
    grad_total = jnp.concatenate(
        [
            lax.dot_general(x_rows, act_rows, contract_rows, preferred_element_type=jnp.float32),
            lax.dot_general(dy_rows, h_rows, contract_rows, preferred_element_type=jnp.float32),
        ],
        1,
    )
    dx_back = lax.all_to_all(
        spread(dx_rows, back_rows, live_back, owners, slot_cap),
        "expert",
        split_axis=0,
        concat_axis=0,
        tiled=True,
    )
    y_pairs = y_back.reshape(-1, feat_width)[pair_slots].reshape(tok_rows, top_picks, feat_width)
    dx_pairs = dx_back.reshape(-1, feat_width)[pair_slots].reshape(tok_rows, top_picks, feat_width)
    layer_out = jnp.sum(route_weight[:, :, None] * y_pairs.astype(jnp.float32), 1).astype(
        jnp.bfloat16
    )
    route_grad = jnp.einsum("td,tkd->tk", out_grad, y_pairs, preferred_element_type=jnp.float32)
    token_grad = jnp.sum(dx_pairs.astype(jnp.float32), 1).astype(jnp.bfloat16)
    local_rows = feat_width // lax.axis_size("dp")
    summed = lax.psum(grad_total.astype(jnp.bfloat16), "dp").astype(jnp.float32)
    mine = lax.dynamic_slice_in_dim(summed, lax.axis_index("dp") * local_rows, local_rows, 0)
    gate_grad = mine[:, :hidden_units][None]
    up_grad = mine[:, hidden_units : 2 * hidden_units][None]
    down_grad = mine[:, 2 * hidden_units :].T[None]
    return (layer_out, token_grad, route_grad, gate_grad, up_grad, down_grad)


def solution(mesh):
    placed = (
        P(("dp", "expert"), None),
        P(("dp", "expert"), None),
        P(("dp", "expert"), None),
        P(("dp", "expert"), None),
        P("expert", "dp", None),
        P("expert", "dp", None),
        P("expert", None, "dp"),
    )
    return jax.shard_map(
        shards,
        mesh=mesh,
        in_specs=placed,
        out_specs=(
            P(("dp", "expert"), None),
            P(("dp", "expert"), None),
            P(("dp", "expert"), None),
            P("expert", "dp", None),
            P("expert", "dp", None),
            P("expert", None, "dp"),
        ),
        check_vma=False,
    )
```

profile of v0, /device:TPU:2, one launch (start us, length us, event | category | flops | bytes accessed | tf_op | source)
XLA Modules:
  0.0 552.6 jit_solution(12986864640239789348)
XLA Ops:
  7.2 0.8 copy.47
  8.2 1.2 reduce-window.11
  9.8 0.7 copy.48
  10.6 18.6 %all-to-all-start = ((s32[64,1,1]{2,1,0:T(1,128)}), s32[64,1,1]{2,1,0:T(1,128)S(1)}, u32[]{:S(2)}, u32[]{:S(2)}) async-start(s32[64,1,1]{2,1,0:T(1,128)} %copy.48), calls=%async_computation | async-start | bytes 65536 | tf_op jit(solution)/shard_map/all_to_all | solution.py:77
  30.1 0.8 copy.46
  31.6 0.9 convert_element_type.52
  32.5 3.0 scatter_custom_fusion.1
  35.5 1.6 reshape.248
  37.1 5.6 %all-to-all-done = s32[64,1,1]{2,1,0:T(1,128)S(1)} async-done(((s32[64,1,1]{2,1,0:T(1,128)}), s32[64,1,1]{2,1,0:T(1,128)S(1)}, u32[]{:S(2)}, u32[]{:S(2)}) %all-to-all-start) | async-done | bytes 288 | tf_op jit(solution)/shard_map/all_to_all | solution.py:77
  42.7 9.5 %all-to-all-start.3 = ((bf16[64,10,1024]{2,1,0:T(8,128)(2,1)}), bf16[64,10,1024]{2,1,0:T(8,128)(2,1)S(1)}, u32[]{:S(2)}, u32[]{:S(2)}) async-start(bf16[64,10,1024]{2,1,0:T(8,128)(2,1)} %reshape.248), calls=%async_computation.3 | async-start | bytes 4194304 | tf_op jit(solution)/shard_map/all_to_all | solution.py:112
  52.2 3.7 scatter_custom_fusion
  55.9 3.6 reshape.242
  59.5 90.4 %all-to-all-done.3 = bf16[64,10,1024]{2,1,0:T(8,128)(2,1)S(1)} async-done(((bf16[64,10,1024]{2,1,0:T(8,128)(2,1)}), bf16[64,10,1024]{2,1,0:T(8,128)(2,1)S(1)}, u32[]{:S(2)}, u32[]{:S(2)}) %all-to-all-start.3) | async-done | bytes 1310752 | tf_op jit(solution)/shard_map/all_to_all | solution.py:112
  149.9 7.5 %all-to-all-start.1 = ((bf16[64,10,1024]{2,1,0:T(8,128)(2,1)}), bf16[64,10,1024]{2,1,0:T(8,128)(2,1)}, u32[]{:S(2)}, u32[]{:S(2)}) async-start(bf16[64,10,1024]{2,1,0:T(8,128)(2,1)} %reshape.242), calls=%async_computation.1 | async-start | bytes 4194304 | tf_op jit(solution)/shard_map/all_to_all | solution.py:76
  157.5 13.9 %all_gather.9 = bf16[1,1024,384]{2,1,0:T(8,128)(2,1)S(1)} all-gather(bf16[1,128,384]{2,1,0:T(8,128)(2,1)S(1)} %copy-done.13), channel_id=1, replica_groups=mesh['dp'=8,'expert'=64] {'dp'}, dimensions={1}, use_global_device_ids=true | all-gather | bytes 884736 | tf_op jit(solution)/shard_map/all_gather | solution.py:68
  171.4 13.4 %all_gather.10 = bf16[1,1024,384]{2,1,0:T(8,128)(2,1)S(1)} all-gather(bf16[1,128,384]{2,1,0:T(8,128)(2,1)S(1)} %copy-done.14), channel_id=1, replica_groups=mesh['dp'=8,'expert'=64] {'dp'}, dimensions={1}, use_global_device_ids=true | all-gather | bytes 884736 | tf_op jit(solution)/shard_map/all_gather | solution.py:69
  184.8 14.1 %all_gather.11 = bf16[1,384,1024]{2,1,0:T(8,128)(2,1)} all-gather(bf16[1,384,128]{2,1,0:T(8,128)(2,1)S(1)} %copy-done.15), channel_id=1, replica_groups=mesh['dp'=8,'expert'=64] {'dp'}, dimensions={2}, use_global_device_ids=true | all-gather | bytes 884736 | tf_op jit(solution)/shard_map/all_gather | solution.py:70
  200.3 1.2 reduce.1
  203.7 2.6 reshape.249
  206.2 3.5 gather_fusion.3
  209.7 45.1 %all-to-all-done.1 = bf16[64,10,1024]{2,1,0:T(8,128)(2,1)} async-done(((bf16[64,10,1024]{2,1,0:T(8,128)(2,1)}), bf16[64,10,1024]{2,1,0:T(8,128)(2,1)}, u32[]{:S(2)}, u32[]{:S(2)}) %all-to-all-start.1) | async-done | bytes 1310752 | tf_op jit(solution)/shard_map/all_to_all | solution.py:76
  254.8 2.6 reshape.243
  257.4 3.5 gather_fusion
  260.9 3.5 broadcast_select_fusion.2
  264.5 1.1 broadcast.188
  265.5 1.0 broadcast.188.clone
  266.6 17.2 %while.28 = (s32[]{:T(128)}, bf16[640,1024]{1,0:T(8,128)(2,1)S(1)}, bf16[640,384]{1,0:T(8,128)(2,1)S(1)}, f32[640,384]{1,0:T(8,128)}, f32[640,384]{1,0:T(8,128)}...) while((s32[]{:T(128)}, bf16[640,1024]{1,0:T(8,128)(2,1)S(1)}, ...), condition=%wide.region_9.10_spmd, body=%wide.region_8.9_spmd.sunk | while | flops 302415872 | bytes 7768279 | solution.py:104
  266.6 2.0 constant_dynamic-update-slice_fusion.6
  268.6 1.3 constant_dynamic-update-slice_fusion.7
  270.9 2.0 constant_dynamic-update-slice_fusion.6
  272.9 1.3 constant_dynamic-update-slice_fusion.7
  275.2 2.0 constant_dynamic-update-slice_fusion.6
  277.2 1.3 constant_dynamic-update-slice_fusion.7
  279.5 2.0 constant_dynamic-update-slice_fusion.6
  281.5 1.3 constant_dynamic-update-slice_fusion.7
  283.8 0.9 copy-done.1
  285.0 1.0 broadcast_in_dim.88
  286.1 13.1 %while.29 = (s32[]{:T(128)}, bf16[640,1024]{1,0:T(8,128)(2,1)S(1)}, bf16[640,768]{1,0:T(8,128)(2,1)}, s32[]{:T(128)}, bf16[640,1024]{1,0:T(8,128)(2,1)}, /*index...) while((s32[]{:T(128)}, bf16[640,1024]{1,0:T(8,128)(2,1)S(1)}, ...), condition=%wide.region_13.14_spmd, body=%wide.region_12.13_spmd.sunk | while | flops 303284224 | bytes 8258775 | solution.py:145
  286.1 1.8 multiply_convert_fusion.5
  289.3 1.8 multiply_convert_fusion.5
  291.9 0.7 maximum_dynamic-update-slice_fusion.2
  292.6 1.8 multiply_convert_fusion.5
  295.9 1.8 multiply_convert_fusion.5
  299.1 3.5 gather_fusion.4
  302.6 3.6 gather.28
  306.2 3.5 gather_fusion.1
  309.7 3.7 gather.24
  313.5 3.3 broadcast_select_fusion
  316.7 112.2 %all_to_all.32 = bf16[64,10,1024]{2,1,0:T(8,128)(2,1)} all-to-all(bf16[64,10,1024]{2,1,0:T(8,128)(2,1)S(1)} %get-tuple-element.204), channel_id=1, replica_groups=mesh['dp'=8,'expert'=64] {'expert'}, dimensions={0} | all-to-all | bytes 2621440 | tf_op jit(solution)/shard_map/all_to_all | solution.py:153
  429.0 9.0 %all-to-all-start.2 = ((bf16[64,10,1024]{2,1,0:T(8,128)(2,1)}), bf16[64,10,1024]{2,1,0:T(8,128)(2,1)}, u32[]{:S(2)}, u32[]{:S(2)}) async-start(bf16[64,10,1024]{2,1,0:T(8,128)(2,1)} %get-tuple-element.205), calls=%async_computation.2 | async-start | bytes 4194304 | tf_op jit(solution)/shard_map/all_to_all | solution.py:105
  438.3 0.8 convolution_convert_fusion.2
  439.6 2.6 convolution_convert_fusion.1
  442.3 1.7 pad_maximum_fusion
  444.0 85.1 %all-reduce.2.cloned.1.call-done = bf16[1024,1152]{0,1:T(8,128)(2,1)} async-done(((bf16[1024,1152]{0,1:T(8,128)(2,1)}), bf16[1024,1152]{0,1:T(8,128)(2,1)}) %all-reduce.2.cloned.1.call-update) | async-done | bytes 2359312 | tf_op jit(solution)/shard_map/psum | solution.py:168
  529.1 1.0 dynamic-slice_convert_fusion
  530.1 0.7 slice_bitcast_fusion
  530.8 0.8 copy.54
  531.6 0.8 copy.55
  532.4 2.6 reshape.250
  535.0 2.1 gather_fusion.5
  537.1 1.4 bitcast_reduce_fusion
  538.4 2.6 reshape.246
  541.0 2.1 gather_fusion.2
  543.1 1.3 multiply_reduce_fusion
  (100 shorter events, 16.9 us)
Async XLA Ops:
  7.2 45.0 %copy-start = (bf16[64,1024]{1,0:T(8,128)(2,1)S(1)}, bf16[64,1024]{1,0:T(8,128)(2,1)}, u32[]{:S(2)}) copy-start(bf16[64,1024]{1,0:T(8,128)(2,1)} %param.11) | copy-start | bytes 393220
  10.6 32.1 %all-to-all-start = ((s32[64,1,1]{2,1,0:T(1,128)}), s32[64,1,1]{2,1,0:T(1,128)S(1)}, u32[]{:S(2)}, u32[]{:S(2)}) async-start(s32[64,1,1]{2,1,0:T(1,128)} %copy.48), calls=%async_computation | async-start | bytes 65536 | tf_op jit(solution)/shard_map/all_to_all | solution.py:77
  30.9 0.6 copy-start.10
  42.7 107.2 %all-to-all-start.3 = ((bf16[64,10,1024]{2,1,0:T(8,128)(2,1)}), bf16[64,10,1024]{2,1,0:T(8,128)(2,1)S(1)}, u32[]{:S(2)}, u32[]{:S(2)}) async-start(bf16[64,10,1024]{2,1,0:T(8,128)(2,1)} %reshape.248), calls=%async_computation.3 | async-start | bytes 4194304 | tf_op jit(solution)/shard_map/all_to_all | solution.py:112
  59.5 98.0 %copy-start.13 = (bf16[1,128,384]{2,1,0:T(8,128)(2,1)S(1)}, bf16[1,128,384]{2,1,0:T(8,128)(2,1)}, u32[]{:S(2)}) copy-start(bf16[1,128,384]{2,1,0:T(8,128)(2,1)} %param.15) | copy-start | bytes 294916
  59.5 111.9 %copy-start.14 = (bf16[1,128,384]{2,1,0:T(8,128)(2,1)S(1)}, bf16[1,128,384]{2,1,0:T(8,128)(2,1)}, u32[]{:S(2)}) copy-start(bf16[1,128,384]{2,1,0:T(8,128)(2,1)} %param.16) | copy-start | bytes 294916
  149.9 7.6 %copy-start.5 = (bf16[64,10,1024]{2,1,0:T(8,128)(2,1)}, bf16[64,10,1024]{2,1,0:T(8,128)(2,1)S(1)}, u32[]{:S(2)}) copy-start(bf16[64,10,1024]{2,1,0:T(8,128)(2,1)S(1)} %all-to-all-done.3) | copy-start | bytes 3932164
  149.9 104.9 %all-to-all-start.1 = ((bf16[64,10,1024]{2,1,0:T(8,128)(2,1)}), bf16[64,10,1024]{2,1,0:T(8,128)(2,1)}, u32[]{:S(2)}, u32[]{:S(2)}) async-start(bf16[64,10,1024]{2,1,0:T(8,128)(2,1)} %reshape.242), calls=%async_computation.1 | async-start | bytes 4194304 | tf_op jit(solution)/shard_map/all_to_all | solution.py:76
  157.4 27.3 %copy-start.15 = (bf16[1,384,128]{2,1,0:T(8,128)(2,1)S(1)}, bf16[1,384,128]{2,1,0:T(8,128)(2,1)}, u32[]{:S(2)}) copy-start(bf16[1,384,128]{2,1,0:T(8,128)(2,1)} %param.17) | copy-start | bytes 294916
  266.6 3.3 copy-start.3
  270.9 3.3 copy-start.3
  275.2 3.3 copy-start.3
  279.5 3.3 copy-start.3
  283.8 0.9 copy-start.1
  283.8 1.1 copy-start.8
  286.1 2.2 copy-start.2
  289.3 2.2 copy-start.2
  292.6 2.2 copy-start.2
  295.9 2.2 copy-start.2
  309.7 3.7 copy-start.4
  429.0 9.3 %copy-start.7 = (bf16[640,1024]{1,0:T(8,128)(2,1)S(1)}, bf16[640,1024]{1,0:T(8,128)(2,1)}, u32[]{:S(2)}) copy-start(bf16[640,1024]{1,0:T(8,128)(2,1)} %get-tuple-element.444) | copy-start | bytes 3932164
  429.0 9.3 %copy-start.9 = (bf16[640,384]{1,0:T(8,128)(2,1)S(1)}, bf16[640,384]{1,0:T(8,128)(2,1)}, u32[]{:S(2)}) copy-start(bf16[640,384]{1,0:T(8,128)(2,1)} %copy-done.8) | copy-start | bytes 1474564
  429.0 109.5 %all-to-all-start.2 = ((bf16[64,10,1024]{2,1,0:T(8,128)(2,1)}), bf16[64,10,1024]{2,1,0:T(8,128)(2,1)}, u32[]{:S(2)}, u32[]{:S(2)}) async-start(bf16[64,10,1024]{2,1,0:T(8,128)(2,1)} %get-tuple-element.205), calls=%async_computation.2 | async-start | bytes 4194304 | tf_op jit(solution)/shard_map/all_to_all | solution.py:105
  438.0 91.1 %all-reduce.2.cloned.1.call-start = ((), (), s32[]{:S(2)}) async-start(), calls=%async_computation.5 | async-start | bytes 4718592 | tf_op jit(solution)/shard_map/psum | solution.py:168
  438.3 1.3 copy-start.6
  541.0 2.1 copy-start.11
  541.0 3.4 copy-start.12
Sparse Core Ops, SparseCore 0:
  444.1 84.9 all-reduce.1
where the time goes:
time: 554 us; the launch traced here: 553 us
  waiting for transfers between devices  226 us (41%)
  blocking collectives  154 us (28%)
  local copies, waits for them, and re-layouts  60 us (11%)
  starting transfers between devices  45 us (8%)
  matrix products  28.5 us (5%)
  other arithmetic  24 us (4%)
  between operations  15.1 us (3%)
    all_to_all x1, blocking collectives, shards(): lax.all_to_all(spread(dx_rows, back_rows, live_back, owners, slot_cap), '...  112 us
    all_to_all x1, waiting for transfers between devices, shards(): lax.all_to_all(dy_send, 'expert', split_axis=0, concat_axis=0, tiled=True)  90.4 us
    psum x1, waiting for transfers between devices, shards(): summed = lax.psum(grad_total.astype(jnp.bfloat16), 'dp').astype(jnp.float32)  85.1 us
    all_to_all x1, waiting for transfers between devices, shards(): lax.all_to_all(x_send, 'expert', split_axis=0, concat_axis=0, tiled=True)  45.1 us
    all_to_all x1, starting transfers between devices, shards(): lax.all_to_all(send_counts, 'expert', split_axis=0, concat_axis=0, tiled=...  18.6 us
    gather x4, local copies, waits for them, and re-layouts, spread(): picked = rows[back_rows]  14.3 us
    all_gather x1, blocking collectives, shards(): lax.all_gather(down_weight, 'dp', axis=2, tiled=True)  14.1 us
    all_gather x1, blocking collectives, shards(): lax.all_gather(gate_weight, 'dp', axis=1, tiled=True)  13.9 us
  transfers between devices with their start and end apart: 5, of which 4 were waited for; matrix products, arithmetic and copies ran while one was open for 7% of the time, Pallas kernels for 0%

commit v1 on v0

--- a/solution.py
+++ b/solution.py
@@ -2,6 +2,12 @@
 import jax.numpy as jnp
 from jax import lax
 from jax.sharding import PartitionSpec as P
+
+
+def add_all(shard, name):
+    terms = lax.all_gather(shard, name, axis=0, tiled=False)
+    acc = terms.sum(axis=0)
+    return acc
 
 
 def layout(live_counts, slot_cap, padded_rows):
@@ -165,7 +171,7 @@
     route_grad = jnp.einsum("td,tkd->tk", out_grad, y_pairs, preferred_element_type=jnp.float32)
     token_grad = jnp.sum(dx_pairs.astype(jnp.float32), 1).astype(jnp.bfloat16)
     local_rows = feat_width // lax.axis_size("dp")
-    summed = lax.psum(grad_total.astype(jnp.bfloat16), "dp").astype(jnp.float32)
+    summed = add_all(grad_total.astype(jnp.bfloat16), "dp").astype(jnp.float32)
     mine = lax.dynamic_slice_in_dim(summed, lax.axis_index("dp") * local_rows, local_rows, 0)
     gate_grad = mine[:, :hidden_units][None]
     up_grad = mine[:, hidden_units : 2 * hidden_units][None]

time: 554 us -> 576 us (1.040)
  the two profiles are of different devices: /device:TPU:2 before, /device:TPU:38 now
where the time goes in v1:
time: 576 us; the launch traced here: 575 us
  waiting for transfers between devices  234 us (41%)
  blocking collectives  146 us (25%)
  local copies, waits for them, and re-layouts  61.1 us (11%)
  starting transfers between devices  44.2 us (8%)
  matrix products  39.1 us (7%)
  other arithmetic  35.4 us (6%)
  between operations  15.1 us (3%)
    all_to_all x1, blocking collectives, shards(): lax.all_to_all(spread(y_rows, back_rows, live_back, owners, slot_cap), 'e...  104 us
    all_to_all x1, waiting for transfers between devices, shards(): lax.all_to_all(spread(dx_rows, back_rows, live_back, owners, slot_cap), '...  92.6 us
    all_to_all x1, waiting for transfers between devices, shards(): lax.all_to_all(dy_send, 'expert', split_axis=0, concat_axis=0, tiled=True)  90.1 us
    all_to_all x1, waiting for transfers between devices, shards(): lax.all_to_all(x_send, 'expert', split_axis=0, concat_axis=0, tiled=True)  45.8 us
    all_to_all x1, starting transfers between devices, shards(): lax.all_to_all(send_counts, 'expert', split_axis=0, concat_axis=0, tiled=...  18.3 us
    all_gather x1, blocking collectives, shards(): lax.all_gather(down_weight, 'dp', axis=2, tiled=True)  14.8 us
    all_gather x1, blocking collectives, shards(): lax.all_gather(up_weight, 'dp', axis=1, tiled=True)  13.6 us
    all_gather x1, blocking collectives, shards(): lax.all_gather(gate_weight, 'dp', axis=1, tiled=True)  13.4 us
  transfers between devices with their start and end apart: 5, of which 4 were waited for; matrix products, arithmetic and copies ran while one was open for 9% of the time, Pallas kernels for 0%

profile of v1, /device:TPU:38, one launch (start us, length us, event | category | flops | bytes accessed | tf_op | source)
XLA Modules:
  0.0 574.9 jit_solution(8922200266470210533)
XLA Ops:
  7.2 0.8 copy.48
  8.2 1.2 reduce-window.11
  10.6 18.3 %all-to-all-start = ((s32[64,1,1]{2,1,0:T(1,128)}), s32[64,1,1]{2,1,0:T(1,128)S(1)}, u32[]{:S(2)}, u32[]{:S(2)}) async-start(s32[64,1,1]{2,1,0:T(1,128)} %copy.49), calls=%async_computation | async-start | bytes 65536 | tf_op jit(solution)/shard_map/all_to_all | solution.py:83
  29.8 0.9 convert_element_type.61
  30.9 3.0 scatter_custom_fusion.1
  33.9 1.5 reshape.279
  35.4 5.1 all-to-all-done
  40.5 10.0 %all-to-all-start.3 = ((bf16[64,10,1024]{2,1,0:T(8,128)(2,1)}), bf16[64,10,1024]{2,1,0:T(8,128)(2,1)S(1)}, u32[]{:S(2)}, u32[]{:S(2)}) async-start(bf16[64,10,1024]{2,1,0:T(8,128)(2,1)} %reshape.279), calls=%async_computation.3 | async-start | bytes 4194304 | tf_op jit(solution)/shard_map/all_to_all | solution.py:118
  50.6 3.7 scatter_custom_fusion
  54.3 3.6 reshape.273
  57.9 90.1 %all-to-all-done.3 = bf16[64,10,1024]{2,1,0:T(8,128)(2,1)S(1)} async-done(((bf16[64,10,1024]{2,1,0:T(8,128)(2,1)}), bf16[64,10,1024]{2,1,0:T(8,128)(2,1)S(1)}, u32[]{:S(2)}, u32[]{:S(2)}) %all-to-all-start.3) | async-done | bytes 1310752 | tf_op jit(solution)/shard_map/all_to_all | solution.py:118
  148.0 1.3 copy-done.5
  149.3 7.8 %all-to-all-start.1 = ((bf16[64,10,1024]{2,1,0:T(8,128)(2,1)}), bf16[64,10,1024]{2,1,0:T(8,128)(2,1)}, u32[]{:S(2)}, u32[]{:S(2)}) async-start(bf16[64,10,1024]{2,1,0:T(8,128)(2,1)} %reshape.273), calls=%async_computation.1 | async-start | bytes 4194304 | tf_op jit(solution)/shard_map/all_to_all | solution.py:82
  157.2 14.8 %all_gather.15 = bf16[1,384,1024]{2,1,0:T(8,128)(2,1)} all-gather(bf16[1,384,128]{2,1,0:T(8,128)(2,1)S(1)} %copy-done.9), channel_id=1, replica_groups=mesh['dp'=8,'expert'=64] {'dp'}, dimensions={2}, use_global_device_ids=true | all-gather | bytes 884736 | tf_op jit(solution)/shard_map/all_gather | solution.py:76
  172.0 13.4 %all_gather.13 = bf16[1,1024,384]{2,1,0:T(8,128)(2,1)S(1)} all-gather(bf16[1,128,384]{2,1,0:T(8,128)(2,1)S(1)} %copy-done.10), channel_id=1, replica_groups=mesh['dp'=8,'expert'=64] {'dp'}, dimensions={1}, use_global_device_ids=true | all-gather | bytes 884736 | tf_op jit(solution)/shard_map/all_gather | solution.py:74
  185.4 13.6 %all_gather.14 = bf16[1,1024,384]{2,1,0:T(8,128)(2,1)S(1)} all-gather(bf16[1,128,384]{2,1,0:T(8,128)(2,1)S(1)} %copy-done.11), channel_id=1, replica_groups=mesh['dp'=8,'expert'=64] {'dp'}, dimensions={1}, use_global_device_ids=true | all-gather | bytes 884736 | tf_op jit(solution)/shard_map/all_gather | solution.py:75
  200.3 1.2 reduce.2
  203.1 2.6 reshape.280
  205.7 3.5 gather_fusion.3
  209.2 45.8 %all-to-all-done.1 = bf16[64,10,1024]{2,1,0:T(8,128)(2,1)} async-done(((bf16[64,10,1024]{2,1,0:T(8,128)(2,1)}), bf16[64,10,1024]{2,1,0:T(8,128)(2,1)}, u32[]{:S(2)}, u32[]{:S(2)}) %all-to-all-start.1) | async-done | bytes 1310752 | tf_op jit(solution)/shard_map/all_to_all | solution.py:82
  255.0 2.6 reshape.274
  257.6 3.5 gather_fusion
  261.1 3.4 broadcast_select_fusion.2
  264.6 0.8 broadcast_in_dim.82
  265.5 1.0 broadcast.188
  266.5 1.0 broadcast.188.clone
  267.5 24.6 %while.28 = (s32[]{:T(128)}, bf16[640,1024]{1,0:T(8,128)(2,1)S(1)}, bf16[640,384]{1,0:T(8,128)(2,1)}, f32[640,384]{1,0:T(8,128)}, f32[640,384]{1,0:T(8,128)}, /*...) while((s32[]{:T(128)}, bf16[640,1024]{1,0:T(8,128)(2,1)S(1)}, ...), condition=%wide.region_9.10_spmd, body=%wide.region_8.9_spmd.sunk | while | flops 302415872 | bytes 7768287 | solution.py:110
  267.5 2.0 constant_dynamic-update-slice_fusion.6
  269.5 1.9 constant_dynamic-update-slice_fusion.7
  272.4 2.0 constant_dynamic-update-slice_fusion.6
  274.4 1.9 constant_dynamic-update-slice_fusion.7
  277.3 2.0 constant_dynamic-update-slice_fusion.6
  279.3 1.9 constant_dynamic-update-slice_fusion.7
  282.3 2.0 constant_dynamic-update-slice_fusion.6
  284.3 1.9 constant_dynamic-update-slice_fusion.7
  287.2 2.0 constant_dynamic-update-slice_fusion.6
  289.2 1.9 constant_dynamic-update-slice_fusion.7
  292.1 0.9 copy-done.2
  293.1 1.0 broadcast_in_dim.88
  294.2 16.3 %while.29 = (s32[]{:T(128)}, bf16[640,1024]{1,0:T(8,128)(2,1)S(1)}, bf16[640,768]{1,0:T(8,128)(2,1)}, s32[]{:T(128)}, bf16[640,1024]{1,0:T(8,128)(2,1)}, /*index...) while((s32[]{:T(128)}, bf16[640,1024]{1,0:T(8,128)(2,1)S(1)}, ...), condition=%wide.region_13.14_spmd, body=%wide.region_12.13_spmd.sunk | while | flops 303284224 | bytes 8258783 | solution.py:151
  294.2 1.8 multiply_convert_fusion.5
  297.5 1.8 multiply_convert_fusion.5
  300.7 1.8 multiply_convert_fusion.5
  304.0 1.8 multiply_convert_fusion.5
  307.3 1.8 multiply_convert_fusion.5
  310.5 2.4 fusion.14
  312.9 1.5 fusion.13
  314.4 1.6 pad_maximum_fusion
  316.0 4.3 copy.55
  320.9 3.5 gather_fusion.4
  324.4 3.6 gather.28
  328.0 2.8 gather_fusion.1
  330.8 1.6 gather.24
  332.4 4.5 broadcast_select_fusion
  336.9 104.5 %all_to_all.32 = bf16[64,10,1024]{2,1,0:T(8,128)(2,1)} all-to-all(bf16[64,10,1024]{2,1,0:T(8,128)(2,1)S(1)} %get-tuple-element.180), channel_id=1, replica_groups=mesh['dp'=8,'expert'=64] {'expert'}, dimensions={0} | all-to-all | bytes 2621440 | tf_op jit(solution)/shard_map/all_to_all | solution.py:111
  441.4 8.0 %all-to-all-start.4 = ((bf16[64,10,1024]{2,1,0:T(8,128)(2,1)}), bf16[64,10,1024]{2,1,0:T(8,128)(2,1)S(1)}, u32[]{:S(2)}, u32[]{:S(2)}) async-start(bf16[64,10,1024]{2,1,0:T(8,128)(2,1)} %get-tuple-element.179), calls=%async_computation.4 | async-start | bytes 4194304 | tf_op jit(solution)/shard_map/all_to_all | solution.py:159
  449.4 2.6 reshape.277
  452.0 2.8 gather_fusion.2
  454.8 92.6 %all-to-all-done.4 = bf16[64,10,1024]{2,1,0:T(8,128)(2,1)S(1)} async-done(((bf16[64,10,1024]{2,1,0:T(8,128)(2,1)}), bf16[64,10,1024]{2,1,0:T(8,128)(2,1)S(1)}, u32[]{:S(2)}, u32[]{:S(2)}) %all-to-all-start.4) | async-done | bytes 1310752 | tf_op jit(solution)/shard_map/all_to_all | solution.py:159
  547.9 2.1 gather_fusion.5
  550.0 1.6 fusion.17
  552.2 1.4 bitcast_reduce_fusion
  553.6 1.3 multiply_reduce_fusion
  554.9 10.4 %reduce_sum.81 = bf16[1024,1152]{1,0:T(8,128)(2,1)S(1)} reduce(bf16[8,1024,1152]{2,1,0:T(8,128)(2,1)} %all-gather.2.cloned.1.call-done, bf16[]{:T(256)} %constant.74.clone.1), dimensions={0}, to_apply=%region_15.16 | reduce | flops 8257536 | bytes 21233666 | tf_op jit(solution)/shard_map/reduce_sum | solution.py:9
  (111 shorter events, 21.8 us)
Async XLA Ops:
  7.2 43.4 %copy-start = (bf16[64,1024]{1,0:T(8,128)(2,1)S(1)}, bf16[64,1024]{1,0:T(8,128)(2,1)}, u32[]{:S(2)}) copy-start(bf16[64,1024]{1,0:T(8,128)(2,1)} %param.11) | copy-start | bytes 393220
  7.2 23.6 %copy-start.12 = (f32[64,8]{0,1:T(8,128)S(1)}, f32[64,8]{0,1:T(8,128)}, u32[]{:S(2)}) copy-start(f32[64,8]{0,1:T(8,128)} %param.13) | copy-start | bytes 6148
  10.6 30.0 %all-to-all-start = ((s32[64,1,1]{2,1,0:T(1,128)}), s32[64,1,1]{2,1,0:T(1,128)S(1)}, u32[]{:S(2)}, u32[]{:S(2)}) async-start(s32[64,1,1]{2,1,0:T(1,128)} %copy.49), calls=%async_computation | async-start | bytes 65536 | tf_op jit(solution)/shard_map/all_to_all | solution.py:83
  40.5 107.4 %all-to-all-start.3 = ((bf16[64,10,1024]{2,1,0:T(8,128)(2,1)}), bf16[64,10,1024]{2,1,0:T(8,128)(2,1)S(1)}, u32[]{:S(2)}, u32[]{:S(2)}) async-start(bf16[64,10,1024]{2,1,0:T(8,128)(2,1)} %reshape.279), calls=%async_computation.3 | async-start | bytes 4194304 | tf_op jit(solution)/shard_map/all_to_all | solution.py:118
  57.9 99.4 %copy-start.9 = (bf16[1,384,128]{2,1,0:T(8,128)(2,1)S(1)}, bf16[1,384,128]{2,1,0:T(8,128)(2,1)}, u32[]{:S(2)}) copy-start(bf16[1,384,128]{2,1,0:T(8,128)(2,1)} %param.17) | copy-start | bytes 294916
  57.9 114.1 %copy-start.10 = (bf16[1,128,384]{2,1,0:T(8,128)(2,1)S(1)}, bf16[1,128,384]{2,1,0:T(8,128)(2,1)}, u32[]{:S(2)}) copy-start(bf16[1,128,384]{2,1,0:T(8,128)(2,1)} %param.15) | copy-start | bytes 294916
  148.0 1.3 copy-start.5
  149.3 105.7 %all-to-all-start.1 = ((bf16[64,10,1024]{2,1,0:T(8,128)(2,1)}), bf16[64,10,1024]{2,1,0:T(8,128)(2,1)}, u32[]{:S(2)}, u32[]{:S(2)}) async-start(bf16[64,10,1024]{2,1,0:T(8,128)(2,1)} %reshape.273), calls=%async_computation.1 | async-start | bytes 4194304 | tf_op jit(solution)/shard_map/all_to_all | solution.py:82
  157.1 28.2 %copy-start.11 = (bf16[1,128,384]{2,1,0:T(8,128)(2,1)S(1)}, bf16[1,128,384]{2,1,0:T(8,128)(2,1)}, u32[]{:S(2)}) copy-start(bf16[1,128,384]{2,1,0:T(8,128)(2,1)} %param.16) | copy-start | bytes 294916
  157.2 397.8 %all-gather.2.cloned.1.call-start = ((), (), s32[]{:S(2)}) async-start(), calls=%async_computation.5 | async-start | bytes 21233664 | tf_op jit(solution)/shard_map/all_gather | solution.py:8
  267.5 3.9 copy-start.4
  272.4 3.9 copy-start.4
  277.3 3.9 copy-start.4
  282.3 3.9 copy-start.4
  287.2 3.9 copy-start.4
  292.1 0.9 copy-start.2
  294.2 2.2 copy-start.3
  297.4 2.2 copy-start.3
  300.7 2.2 copy-start.3
  304.0 2.2 copy-start.3
  307.3 2.2 copy-start.3
  310.5 2.4 copy-start.6
  310.5 2.4 copy-start.8
  441.4 106.0 %all-to-all-start.4 = ((bf16[64,10,1024]{2,1,0:T(8,128)(2,1)}), bf16[64,10,1024]{2,1,0:T(8,128)(2,1)S(1)}, u32[]{:S(2)}, u32[]{:S(2)}) async-start(bf16[64,10,1024]{2,1,0:T(8,128)(2,1)} %get-tuple-element.179), calls=%async_computation.4 | async-start | bytes 4194304 | tf_op jit(solution)/shard_map/all_to_all | solution.py:159
  547.9 2.1 copy-start.7
  565.4 2.6 copy-start.1
Sparse Core Ops, SparseCore 0:
  320.5 94.4 all-gather.1
